TPU v7x, 256 devices: a whole 4x4x8 slice. The times are simulated.
256 devices in a mesh: dp: 8 (over x, z_hi), context: 32 (over y, z_lo, core).
Axes of the slice: x: 4, y: 4, z: 8 (z_hi: 2, z_lo: 4; z = z_hi * 4 + z_lo), core: 2. Of those that a mesh axis runs over, the one named last changes fastest.
Arguments:
- grad_out: bfloat16 [8, 4096, 4096], P('dp', 'context'), may hold values from -6 to 6
- attn: bfloat16 [8, 4096, 4096], P('dp', 'context'), may hold values from -0.032958984 to 0.032958984
- w_out: bfloat16 [4096, 4096], P('context'), may hold values from -0.09375 to 0.09375
Outputs:
- grad_attn: bfloat16 [8, 4096, 4096], P('dp', None, 'context')
- grad_w: bfloat16 [4096, 4096], P('context')
All inputs are finite; a program needn't handle non-finite values.
Results may differ from a plain program's by a relative error of at most 0.013.
Values may be sent and summed in bfloat16 or wider, within the bound.
No kernel may reach another device: no remote copies, remote signals or barrier semaphores. Data moves between devices by JAX's collectives and lax.ppermute only.
A program may use at most 128 MiB of HBM per device.

v0:
```python
import jax
import jax.numpy as jnp
from jax import lax
from jax.sharding import PartitionSpec as P


def accumulate(heads_view, weight_cols, block_rows):
    local_part = lax.dot_general(
        block_rows, weight_cols, (((1,), (1,)), ((), ())), preferred_element_type=jnp.float32
    )
    weight_acc = lax.dot_general(
        heads_view, block_rows, (((0,), (0,)), ((), ())), preferred_element_type=jnp.float32
    )
    return (local_part, weight_acc)


def local(grad_out, attn, w_out):
    cotangent = grad_out[0]
    activations = attn[0]
    heads_view = lax.all_to_all(activations, "context", split_axis=1, concat_axis=0, tiled=True)
    head_acc, weight_acc = accumulate(
        heads_view, w_out, lax.all_gather(cotangent, "context", axis=0, tiled=True)
    )
    weight_sum = lax.psum(weight_acc.astype(jnp.bfloat16), "dp")
    return (head_acc.astype(jnp.bfloat16)[None], weight_sum)


def solution(mesh):
    in_specs = (P("dp", "context", None), P("dp", "context", None), P("context", None))
    out_specs = (P("dp", None, "context"), P("context", None))
    return jax.shard_map(local, mesh=mesh, in_specs=in_specs, out_specs=out_specs, check_vma=False)
```

profile of v0, /device:TPU:1, one launch (start us, length us, event | category | flops | bytes accessed | tf_op | source)
XLA Modules:
  0.0 370.2 jit_solution(1322192716840169379)
XLA Ops:
  7.2 0.0 copy-start
  7.2 0.0 all-gather.3.cloned.1.call-start
  7.2 0.7 all-gather.3.cloned.1.call-update
  7.9 0.0 all-reduce.2.cloned.1.call-start
  8.0 1.6 copy.5
  9.6 45.5 %all_to_all.19 = bf16[128,32,128]{0,2,1:T(8,128)(2,1)S(1)} all-to-all(bf16[128,32,128]{0,2,1:T(8,128)(2,1)S(1)} %bitcast.20), channel_id=1, replica_groups=mesh['dp'=8,'context'=32] {'context'}, dimensions={1} | all-to-all | bytes 2097152 | tf_op jit(solution)/shard_map/all_to_all | solution.py:20
  55.1 0.7 copy.6
  55.8 154.1 %all-gather.3.cloned.1.call-done = bf16[1,4096,4096]{2,1,0:T(8,128)(2,1)} async-done(((bf16[1,128,4096]{2,1,0:T(8,128)(2,1)}), bf16[1,4096,4096]{2,1,0:T(8,128)(2,1)}) %all-gather.3.cloned.1.call-update) | async-done | bytes 33554448 | tf_op jit(solution)/shard_map/all_gather | solution.py:22
  209.9 14.0 %fusion.7 = bf16[128,4096]{1,0:T(8,128)(2,1)} fusion(bf16[4096,128]{1,0:T(8,128)(2,1)S(1)} %bitcast.18, bf16[1,4096,4096]{2,1,0:T(8,128)(2,1)} %all-gather.3.cloned.1.call-done), kind=kOutput, calls=%fused_computation.5 | convolution fusion | flops 4295491584 | bytes 35651584 | tf_op jit(solution)/shard_map/dot_general | solution.py:11
  223.9 0.0 all-reduce.2.cloned.1.call-update
  223.9 0.0 copy-done
  223.9 16.2 %fusion.10 = bf16[1,4096,128]{2,1,0:T(8,128)(2,1)} fusion(bf16[128,4096]{1,0:T(8,128)(2,1)S(1)} %copy-done, bf16[1,4096,4096]{2,1,0:T(8,128)(2,1)} %all-gather.3.cloned.1.call-done), kind=kOutput, calls=%fused_computation.6 | convolution fusion | flops 4295491584 | bytes 35651584 | tf_op jit(solution)/shard_map/dot_general | solution.py:8
  240.1 121.1 %all-reduce.2.cloned.1.call-done = bf16[128,4096]{1,0:T(8,128)(2,1)} async-done(((bf16[128,4096]{1,0:T(8,128)(2,1)}), bf16[128,4096]{1,0:T(8,128)(2,1)}) %all-reduce.2.cloned.1.call-update) | async-done | bytes 1048592 | tf_op jit(solution)/shard_map/psum | solution.py:24
  361.1 2.3 copy.8
Async XLA Ops:
  7.2 216.7 %copy-start = (bf16[128,4096]{1,0:T(8,128)(2,1)S(1)}, bf16[128,4096]{1,0:T(8,128)(2,1)}, u32[]{:S(2)}) copy-start(bf16[128,4096]{1,0:T(8,128)(2,1)} %param.5) | copy-start | bytes 3145732
  7.2 202.7 %all-gather.3.cloned.1.call-start = ((), (), s32[]{:S(2)}) async-start(), calls=%async_computation.2 | async-start | bytes 34603008 | tf_op jit(solution)/shard_map/all_gather | solution.py:22
  7.9 353.2 %all-reduce.2.cloned.1.call-start = ((), (), s32[]{:S(2)}) async-start(), calls=%async_computation.1 | async-start | bytes 2097152 | tf_op jit(solution)/shard_map/psum | solution.py:24
Sparse Core Ops, SparseCore 0:
  9.9 199.9 all-gather.2
  224.0 137.0 all-reduce.1
where the time goes:
time: 370 us
  waiting for transfers between devices  276 us (75%)
  blocking collectives  45.5 us (12%)
  matrix products  30.2 us (8%)
  between operations  14.1 us (4%)
  local copies, waits for them, and re-layouts  4.57 us (1%)
    all_gather x1, waiting for transfers between devices, local(): lax.all_gather(cotangent, 'context', axis=0, tiled=True)  154 us
    psum x1, waiting for transfers between devices, local(): weight_sum = lax.psum(weight_acc.astype(jnp.bfloat16), 'dp')  121 us
    all_to_all x1, blocking collectives, local(): lax.all_to_all(activations, 'context', split_axis=1, concat_axis=0, tiled...  45.5 us
    dot_general x1, matrix products, accumulate(): lax.dot_general(block_rows, weight_cols, (((1,), (1,)), ((), ())), prefer...  16.2 us
    dot_general x1, matrix products, accumulate(): lax.dot_general(heads_view, block_rows, (((0,), (0,)), ((), ())), preferr...  14 us
  transfers between devices with their start and end apart: 2, of which 2 were waited for; matrix products, arithmetic and copies ran while one was open for 5% of the time, Pallas kernels for 0%

commit v1 on v0

--- a/solution.py
+++ b/solution.py
@@ -18,9 +18,14 @@
     cotangent = grad_out[0]
     activations = attn[0]
     heads_view = lax.all_to_all(activations, "context", split_axis=1, concat_axis=0, tiled=True)
-    head_acc, weight_acc = accumulate(
-        heads_view, w_out, lax.all_gather(cotangent, "context", axis=0, tiled=True)
-    )
+
+    def _arrange_targets(tile_in, which_axis):
+        block_now = lax.all_to_all(
+            jnp.stack([tile_in] * lax.axis_size(which_axis), axis=0), which_axis, 0, 0
+        )
+        return jnp.concatenate(block_now, axis=0)
+
+    head_acc, weight_acc = accumulate(heads_view, w_out, _arrange_targets(cotangent, "context"))
     weight_sum = lax.psum(weight_acc.astype(jnp.bfloat16), "dp")
     return (head_acc.astype(jnp.bfloat16)[None], weight_sum)
 

time: 370 us -> 945 us (2.55)
  blocking collectives: 45.5 us -> 769 us
  waiting for transfers between devices: 276 us -> 116 us
  local copies, waits for them, and re-layouts: 4.57 us -> 15.8 us
    all_to_all x0 -> x1, blocking collectives: none -> 731 us  [_arrange_targets(): lax.all_to_all(jnp.stack([tile_in] * lax.axis_size(which_axis), axis=0),...]
    all_gather x1 -> x0, waiting for transfers between devices: 154 us -> none  [local(): lax.all_gather(cotangent, 'context', axis=0, tiled=True)]
    another operation x0 -> x1, local copies, waits for them, and re-layouts: none -> 11.8 us  [_arrange_targets(): jnp.stack([tile_in] * lax.axis_size(which_axis), axis=0)]
  transfers between devices with their start and end apart: 2 -> 1, of which waited for: 2 -> 1; matrix products, arithmetic and copies ran while one was open for 5% -> 2% of each run, Pallas kernels for 0% -> 0%
where the time goes in v1:
time: 945 us
  blocking collectives  769 us (81%)
  waiting for transfers between devices  116 us (12%)
  matrix products  30.4 us (3%)
  local copies, waits for them, and re-layouts  15.8 us (2%)
  between operations  14.1 us (1%)
    all_to_all x1, blocking collectives, _arrange_targets(): lax.all_to_all(jnp.stack([tile_in] * lax.axis_size(which_axis), axis=0),...  731 us
    psum x1, waiting for transfers between devices, local(): weight_sum = lax.psum(weight_acc.astype(jnp.bfloat16), 'dp')  116 us
    all_to_all x1, blocking collectives, local(): lax.all_to_all(activations, 'context', split_axis=1, concat_axis=0, tiled...  37.9 us
  transfers between devices with their start and end apart: 1, of which 1 were waited for; matrix products, arithmetic and copies ran while one was open for 2% of the time, Pallas kernels for 0%

profile of v1, /device:TPU:1, one launch (start us, length us, event | category | flops | bytes accessed | tf_op | source)
XLA Modules:
  0.0 944.7 jit_solution(6084960373157495696)
XLA Ops:
  7.2 0.0 copy-start
  7.2 0.0 all-reduce.2.cloned.1.call-start
  7.2 1.7 copy.5
  8.9 37.9 %all_to_all.21 = bf16[128,32,128]{0,2,1:T(8,128)(2,1)S(1)} all-to-all(bf16[128,32,128]{0,2,1:T(8,128)(2,1)S(1)} %bitcast.16), channel_id=1, replica_groups=mesh['dp'=8,'context'=32] {'context'}, dimensions={1} | all-to-all | bytes 2097152 | tf_op jit(solution)/shard_map/all_to_all | solution.py:20
  46.8 11.8 %stack.3 = bf16[32,128,4096]{2,1,0:T(8,128)(2,1)} broadcast(bf16[128,4096]{1,0:T(8,128)(2,1)} %bitcast.17), dimensions={1,2} | broadcast | bytes 34603008 | tf_op jit(solution)/shard_map/stack | solution.py:24
  58.6 730.8 %all_to_all.22 = bf16[32,128,4096]{2,1,0:T(8,128)(2,1)} all-to-all(bf16[32,128,4096]{2,1,0:T(8,128)(2,1)} %stack.3), channel_id=1, replica_groups=mesh['dp'=8,'context'=32] {'context'}, dimensions={0} | all-to-all | bytes 67108864 | tf_op jit(solution)/shard_map/all_to_all | solution.py:23
  789.4 14.2 %fusion = bf16[128,4096]{1,0:T(8,128)(2,1)} fusion(bf16[32,128,4096]{2,1,0:T(8,128)(2,1)} %all_to_all.22, bf16[128,32,128]{0,2,1:T(8,128)(2,1)S(1)} %all_to_all.21), kind=kOutput, calls=%fused_computation.1 | convolution fusion | flops 4295491584 | bytes 35651584 | tf_op jit(solution)/shard_map/dot_general | solution.py:11
  803.6 0.0 all-reduce.2.cloned.1.call-update
  803.6 0.0 copy-done
  803.6 16.3 %fusion.1 = bf16[1,4096,128]{2,1,0:T(8,128)(2,1)} fusion(bf16[4096,4096]{1,0:T(8,128)(2,1)} %bitcast.15, bf16[128,4096]{1,0:T(8,128)(2,1)S(1)} %copy-done), kind=kOutput, calls=%fused_computation.3 | convolution fusion | flops 4295491584 | bytes 35651584 | tf_op jit(solution)/shard_map/dot_general | solution.py:8
  819.9 115.7 %all-reduce.2.cloned.1.call-done = bf16[128,4096]{1,0:T(8,128)(2,1)} async-done(((bf16[128,4096]{1,0:T(8,128)(2,1)}), bf16[128,4096]{1,0:T(8,128)(2,1)}) %all-reduce.2.cloned.1.call-update) | async-done | bytes 1048592 | tf_op jit(solution)/shard_map/psum | solution.py:29
  935.5 2.3 copy.7
Async XLA Ops:
  7.2 796.5 %copy-start = (bf16[128,4096]{1,0:T(8,128)(2,1)S(1)}, bf16[128,4096]{1,0:T(8,128)(2,1)}, u32[]{:S(2)}) copy-start(bf16[128,4096]{1,0:T(8,128)(2,1)} %param.5) | copy-start | bytes 3145732
  7.2 928.4 %all-reduce.2.cloned.1.call-start = ((), (), s32[]{:S(2)}) async-start(), calls=%async_computation.2 | async-start | bytes 2097152 | tf_op jit(solution)/shard_map/psum | solution.py:29
Sparse Core Ops, SparseCore 0:
  803.7 131.7 all-reduce.1
